TPU v7x, 32 devices: a whole 2x2x4 slice. The times are simulated.
32 devices in a mesh: prow: 4 (over y, x), pcol: 8 (over z, core).
Axes of the slice: x: 2, y: 2, z: 4, core: 2. Of those that a mesh axis runs over, the one named last changes fastest.
Arguments:
- known_inverse: bfloat16 [4096, 4, 8, 128], P('prow', None, 'pcol'), may hold values from -6 to 6
- pattern: int32 [32, 4, 8, 1], P('prow', None, 'pcol'), may hold values 0 or 1
- panel_one: bfloat16 [4096, 512], P(('prow', 'pcol')), may hold values from -0.09375 to 0.09375
- panel_two: bfloat16 [4096, 512], P(('prow', 'pcol')), may hold values from -0.09375 to 0.09375
- panel_top: bfloat16 [512, 512], replicated, may hold values from -0.25 to 0.25
- structure: int32 [4096], P(('prow', 'pcol')), may hold values from 0 to 1, as said below
- diag_one: bfloat16 [512, 512], replicated, may hold values from -6 to 6
- diag_two: bfloat16 [512, 512], replicated, may hold values from -6 to 6
Outputs:
- inverse_one: bfloat16 [4096, 512], P(('prow', 'pcol'))
- corner_one: bfloat16 [512, 512], replicated
- inverse_top: bfloat16 [512, 512], replicated
- inverse_two: bfloat16 [4096, 512], P(('prow', 'pcol'))
- corner_two: bfloat16 [512, 512], replicated
Inputs may be any that keep to these rules, and one draw needn't show every extreme that they name: `structure`: in every aligned pair of rows (2 k and 2 k + 1) at least one entry is 1.
All inputs are finite; a program needn't handle non-finite values. No bound on the sum of `pattern` on one device may be relied on, other than what follows from the above.
Results may differ from a plain program's by a relative error of at most 0.0058.
Values may be sent and summed in bfloat16 or wider, within the bound.
No kernel may reach another device: no remote copies, remote signals or barrier semaphores. Data moves between devices by JAX's collectives and lax.ppermute only.
A program may use at most 128 MiB of HBM per device.

v0:
```python
import jax
import jax.numpy as jnp
from jax import lax
from jax.sharding import PartitionSpec as P

BLK = 128


def on_device(
    known_inverse, pattern, panel_one, panel_two, panel_top, structure, diag_one, diag_two
):
    row_count = known_inverse.shape[0]
    col_groups = known_inverse.shape[1]
    piece_rows = known_inverse.shape[3]
    width = panel_one.shape[1]
    block_rows = row_count // BLK
    piece_blocks = piece_rows // BLK
    shaped = known_inverse.reshape(block_rows, BLK, col_groups, piece_blocks, BLK)
    flag_table = pattern.reshape(block_rows, 1, col_groups, piece_blocks, 1)
    masked = jnp.where(flag_table > 0, shaped, jnp.zeros_like(shaped)).reshape(
        row_count, col_groups * piece_rows
    )
    row_flags = structure.reshape(piece_rows, 1) > 0
    masked_two = jnp.where(row_flags, panel_two, jnp.zeros_like(panel_two))
    partial_both = jnp.dot(
        masked,
        jnp.concatenate(
            (
                lax.all_gather(panel_one, "prow", axis=0, tiled=True),
                lax.all_gather(masked_two, "prow", axis=0, tiled=True),
            ),
            axis=1,
        ),
        preferred_element_type=jnp.float32,
    )
    reduced = lax.psum_scatter(partial_both, "pcol", scatter_dimension=0, tiled=True)
    reduced_one = reduced[:, :width]
    reduced_two = reduced[:, width:]
    inverse_one = (-reduced_one).astype(jnp.bfloat16)
    own_term = jnp.dot(panel_one.T, inverse_one, preferred_element_type=jnp.float32)
    cross_local = jnp.dot(inverse_one.T, masked_two, preferred_element_type=jnp.float32)
    lower_two = -(reduced_two + jnp.dot(inverse_one, panel_top, preferred_element_type=jnp.float32))
    inverse_two = jnp.where(row_flags, lower_two, jnp.zeros_like(lower_two)).astype(jnp.bfloat16)
    tail_local = jnp.dot(masked_two.T, inverse_two, preferred_element_type=jnp.float32)
    top_weights = panel_top.astype(jnp.float32)
    own_sum, cross_sum = lax.psum((own_term, cross_local), ("prow", "pcol"))
    corner_full = diag_one.astype(jnp.float32) - own_sum
    top_value = jnp.dot(corner_full, top_weights, precision=lax.Precision.HIGHEST) + cross_sum
    inverse_top = (-top_value).astype(jnp.bfloat16)
    tail_sum = lax.psum(tail_local, ("prow", "pcol"))
    corner_two = (
        diag_two.astype(jnp.float32)
        - jnp.dot(panel_top.T, inverse_top, preferred_element_type=jnp.float32)
        - tail_sum
    )
    return (
        inverse_one,
        corner_full.astype(jnp.bfloat16),
        inverse_top,
        inverse_two,
        corner_two.astype(jnp.bfloat16),
    )


def solution(mesh):
    in_specs = (
        P("prow", None, "pcol", None),
        P("prow", None, "pcol", None),
        P(("prow", "pcol"), None),
        P(("prow", "pcol"), None),
        P(),
        P(("prow", "pcol")),
        P(),
        P(),
    )
    out_specs = (P(("prow", "pcol"), None), P(), P(), P(("prow", "pcol"), None), P())
    return jax.shard_map(
        on_device, mesh=mesh, in_specs=in_specs, out_specs=out_specs, check_vma=False
    )
```

profile of v0, /device:TPU:0, one launch (start us, length us, event | category | flops | bytes accessed | tf_op | source)
XLA Modules:
  0.0 241.5 jit_solution(9505006935396776031)
XLA Ops:
  7.2 0.0 copy-start
  7.2 0.0 copy-start.11
  7.2 0.0 reduce-scatter.2.cloned.1.call-start
  7.2 0.8 broadcast_compare_fusion.1
  8.0 1.0 broadcast_select_fusion
  9.0 11.5 %all_gather.7 = bf16[512,512]{1,0:T(8,128)(2,1)S(1)} all-gather(bf16[128,512]{1,0:T(8,128)(2,1)S(1)} %broadcast_select_fusion), channel_id=1, replica_groups=mesh['prow'=4,'pcol'=8] {'prow'}, dimensions={0}, use_global_device_ids=true | all-gather | bytes 655360 | tf_op jit(solution)/shard_map/all_gather | solution.py:30
  20.5 0.7 broadcast_compare_fusion
  21.2 0.1 copy.20
  21.3 10.7 %all_gather.6 = bf16[512,512]{1,0:T(8,128)(2,1)S(1)} all-gather(bf16[128,512]{1,0:T(8,128)(2,1)} %param.10), channel_id=1, replica_groups=mesh['prow'=4,'pcol'=8] {'prow'}, dimensions={0}, use_global_device_ids=true | all-gather | bytes 655360 | tf_op jit(solution)/shard_map/all_gather | solution.py:29
  32.0 0.3 broadcast_in_dim.33
  32.4 0.0 copy-done.11
  32.4 3.2 %fusion.8 = f32[1024,1024]{1,0:T(8,128)} fusion(pred[128,8,4,128]{3,2,1,0:T(4,128)(4,1)S(1)} %bitcast.36, bf16[128,8,4,128]{3,2,1,0:T(4,128)(2,1)S(1)} %bitcast.38, bf16[512,512]{1,0:T(8,128)(2,1)S(1)} %all_gather.7, bf16[512,512]{1,0:T(8,128)(2,1)S(1)} %all_gather.6), kind=kOutput, calls=%fused_computation.13 | convolution fusion | flops 1076363264 | bytes 6815744 | tf_op jit(solution)/shard_map/dot_general | solution.py:25
  35.6 0.0 copy-start.6
  35.6 0.0 reduce-scatter.2.cloned.1.call-update
  35.6 0.0 all-reduce.3.cloned.1.call-start
  35.7 50.3 %reduce-scatter.2.cloned.1.call-done = f32[128,1024]{1,0:T(8,128)} async-done(((f32[1024,1024]{1,0:T(8,128)}), f32[128,1024]{1,0:T(8,128)}) %reduce-scatter.2.cloned.1.call-update) | async-done | bytes 524304 | tf_op jit(solution)/shard_map/reduce_scatter | solution.py:36
  86.0 0.0 copy-start.9
  86.0 1.0 fusion.16
  87.0 0.0 copy-start.3
  87.0 1.3 fusion.19
  88.3 0.0 copy-done.6
  88.3 1.3 convolution_bitcast_fusion.1
  89.6 0.0 copy-done
  89.6 0.0 copy-done.9
  89.6 0.2 fusion.7
  89.9 0.0 copy-start.10
  89.9 0.0 copy-start.7
  89.9 1.4 fusion.20
  91.3 0.0 copy-done.3
  91.3 0.0 copy-start.8
  91.3 0.0 all-reduce.3.cloned.1.call-update
  91.3 0.0 copy-done.10
  91.3 0.0 copy-done.7
  91.3 0.2 copy.14
  91.5 0.8 copy-done.8
  92.3 0.2 copy.15
  92.5 136.7 %all-reduce.3.cloned.1.call-done = (f32[512,512]{0,1:T(8,128)}, f32[512,512]{1,0:T(8,128)}, f32[512,512]{0,1:T(8,128)}) async-done(((f32[512,512]{0,1:T(8,128)}, f32[512,512]{1,0:T(8,128)}, f32[512,512]{0,1:T(8,128)}), (f32[512,512]{0,1:T(8,128)}, f32[512,512]{1,0:T(8,128)}, f32[512,512]{0,1:T(8,128)})) %all-reduce.3.cloned.1.call-update) | async-done | bytes 3145744 | tf_op jit(solution)/shard_map/psum | solution.py:46
  229.3 0.0 copy-start.1
  229.3 0.0 copy-start.5
  229.3 1.5 fusion.14
  230.8 0.0 copy-start.4
  230.8 0.0 copy-done.1
  230.8 0.3 copy-done.5
  231.1 1.0 fusion.3
  232.1 0.0 copy-start.2
  232.2 0.0 copy-done.4
  232.2 0.5 fusion.4
  232.6 1.0 copy.18
  233.6 0.0 copy-done.2
  233.7 1.0 copy.17
Async XLA Ops:
  7.2 82.5 %copy-start = (bf16[512,512]{1,0:T(8,128)(2,1)S(1)}, bf16[512,512]{1,0:T(8,128)(2,1)}, u32[]{:S(2)}) copy-start(bf16[512,512]{1,0:T(8,128)(2,1)} %param.12) | copy-start | bytes 1572868
  7.2 25.2 %copy-start.11 = (bf16[1024,4,1,128]{3,1,2,0:T(4,128)(2,1)S(1)}, bf16[1024,4,1,128]{3,1,2,0:T(4,128)(2,1)}, u32[]{:S(2)}) copy-start(bf16[1024,4,1,128]{3,1,2,0:T(4,128)(2,1)} %param.8) | copy-start | bytes 3145732
  7.2 78.8 %reduce-scatter.2.cloned.1.call-start = ((), (), s32[]{:S(2)}) async-start(), calls=%async_computation.1 | async-start | bytes 4718592 | tf_op jit(solution)/shard_map/reduce_scatter | solution.py:36
  35.6 52.7 %copy-start.6 = (bf16[128,512]{1,0:T(8,128)(2,1)S(1)}, bf16[128,512]{1,0:T(8,128)(2,1)}, u32[]{:S(2)}) copy-start(bf16[128,512]{1,0:T(8,128)(2,1)} %param.10) | copy-start | bytes 393220
  35.6 193.6 %all-reduce.3.cloned.1.call-start = ((), (), s32[]{:S(2)}) async-start(), calls=%async_computation.2 | async-start | bytes 6291456 | tf_op jit(solution)/shard_map/psum | solution.py:46
  86.0 3.7 %copy-start.9 = (f32[128,1024]{1,0:T(8,128)S(1)}, f32[128,1024]{1,0:T(8,128)}, u32[]{:S(2)}) copy-start(f32[128,1024]{1,0:T(8,128)} %reduce-scatter.2.cloned.1.call-done) | copy-start | bytes 1572868
  87.0 4.3 %copy-start.3 = (bf16[128,512]{1,0:T(8,128)(2,1)}, bf16[128,512]{1,0:T(8,128)(2,1)S(1)}, u32[]{:S(2)}) copy-start(bf16[128,512]{1,0:T(8,128)(2,1)S(1)} %fusion.16) | copy-start | bytes 393220
  89.9 1.4 copy-start.10
  89.9 1.4 copy-start.7
  91.3 1.0 copy-start.8
  229.3 1.6 copy-start.1
  229.3 1.9 copy-start.5
  230.8 1.4 copy-start.4
  232.1 1.5 copy-start.2
Sparse Core Ops, SparseCore 0:
  35.8 50.1 reduce-scatter.1
  91.8 137.4 all-reduce.2
where the time goes:
time: 242 us; the launch traced here: 241 us
  waiting for transfers between devices  187 us (77%)
  blocking collectives  22.2 us (9%)
  between operations  14.2 us (6%)
  matrix products  8.95 us (4%)
  other arithmetic  5.02 us (2%)
  local copies, waits for them, and re-layouts  4.01 us (2%)
    psum x1, waiting for transfers between devices, on_device(): own_sum, cross_sum = lax.psum((own_term, cross_local), ('prow', 'pcol'))  137 us
    reduce_scatter x1, waiting for transfers between devices, on_device(): lax.psum_scatter(partial_both, 'pcol', scatter_dimension=0, tiled=True)  50.3 us
    all_gather x1, blocking collectives, on_device(): lax.all_gather(masked_two, 'prow', axis=0, tiled=True)  11.5 us
    all_gather x1, blocking collectives, on_device(): lax.all_gather(panel_one, 'prow', axis=0, tiled=True)  10.7 us
  transfers between devices with their start and end apart: 2, of which 2 were waited for; matrix products, arithmetic and copies ran while one was open for 0% of the time, Pallas kernels for 0%

commit v1 on v0

--- a/solution.py
+++ b/solution.py
@@ -4,6 +4,11 @@
 from jax.sharding import PartitionSpec as P
 
 BLK = 128
+
+
+def by_each_axis(value, inner_axis, outer_axis):
+    partial = lax.psum(value, inner_axis)
+    return lax.psum(partial, outer_axis)
 
 
 def on_device(
@@ -43,7 +48,7 @@
     inverse_two = jnp.where(row_flags, lower_two, jnp.zeros_like(lower_two)).astype(jnp.bfloat16)
     tail_local = jnp.dot(masked_two.T, inverse_two, preferred_element_type=jnp.float32)
     top_weights = panel_top.astype(jnp.float32)
-    own_sum, cross_sum = lax.psum((own_term, cross_local), ("prow", "pcol"))
+    own_sum, cross_sum = by_each_axis((own_term, cross_local), "pcol", "prow")
     corner_full = diag_one.astype(jnp.float32) - own_sum
     top_value = jnp.dot(corner_full, top_weights, precision=lax.Precision.HIGHEST) + cross_sum
     inverse_top = (-top_value).astype(jnp.bfloat16)

time: 242 us -> 372 us (1.54)
  waiting for transfers between devices: 187 us -> 317 us
    psum x1 -> x3, waiting for transfers between devices: 137 us -> 266 us  [the longest x1 133 us: on_device(): tail_sum = lax.psum(tail_local, ('prow', 'pcol'))]
  transfers between devices with their start and end apart: 2 -> 4, of which waited for: 2 -> 4; matrix products, arithmetic and copies ran while one was open for 0% -> 1% of each run, Pallas kernels for 0% -> 0%
where the time goes in v1:
time: 372 us
  waiting for transfers between devices  317 us (85%)
  blocking collectives  22.2 us (6%)
  between operations  13.9 us (4%)
  matrix products  10.1 us (3%)
  other arithmetic  4.95 us (1%)
  local copies, waits for them, and re-layouts  3.72 us (1%)
    psum x1, waiting for transfers between devices, on_device(): tail_sum = lax.psum(tail_local, ('prow', 'pcol'))  133 us
    psum x1, waiting for transfers between devices, by_each_axis(): return lax.psum(partial, outer_axis)  69.6 us
    psum x1, waiting for transfers between devices, by_each_axis(): partial = lax.psum(value, inner_axis)  63.8 us
    reduce_scatter x1, waiting for transfers between devices, on_device(): lax.psum_scatter(partial_both, 'pcol', scatter_dimension=0, tiled=True)  50.3 us
    all_gather x1, blocking collectives, on_device(): lax.all_gather(masked_two, 'prow', axis=0, tiled=True)  11.5 us
    all_gather x1, blocking collectives, on_device(): lax.all_gather(panel_one, 'prow', axis=0, tiled=True)  10.7 us
  transfers between devices with their start and end apart: 4, of which 4 were waited for; matrix products, arithmetic and copies ran while one was open for 1% of the time, Pallas kernels for 0%

profile of v1, /device:TPU:0, one launch (start us, length us, event | category | flops | bytes accessed | tf_op | source)
XLA Modules:
  0.0 371.7 jit_solution(2221398023934157617)
XLA Ops:
  7.2 0.0 copy-start
  7.2 0.0 copy-start.10
  7.2 0.0 reduce-scatter.2.cloned.1.call-start
  7.2 0.8 broadcast_compare_fusion.1
  8.0 1.0 broadcast_select_fusion
  9.0 11.5 %all_gather.7 = bf16[512,512]{1,0:T(8,128)(2,1)S(1)} all-gather(bf16[128,512]{1,0:T(8,128)(2,1)S(1)} %broadcast_select_fusion), channel_id=1, replica_groups=mesh['prow'=4,'pcol'=8] {'prow'}, dimensions={0}, use_global_device_ids=true | all-gather | bytes 655360 | tf_op jit(solution)/shard_map/all_gather | solution.py:35
  20.5 0.7 broadcast_compare_fusion
  21.2 0.1 copy.20
  21.3 10.7 %all_gather.6 = bf16[512,512]{1,0:T(8,128)(2,1)S(1)} all-gather(bf16[128,512]{1,0:T(8,128)(2,1)} %param.10), channel_id=1, replica_groups=mesh['prow'=4,'pcol'=8] {'prow'}, dimensions={0}, use_global_device_ids=true | all-gather | bytes 655360 | tf_op jit(solution)/shard_map/all_gather | solution.py:34
  32.0 0.3 broadcast_in_dim.33
  32.4 0.0 copy-done.10
  32.4 3.2 fusion.8
  35.6 0.0 copy-start.5
  35.6 0.0 reduce-scatter.2.cloned.1.call-update
  35.6 0.0 all-reduce.8.cloned.1.call-start
  35.7 50.3 %reduce-scatter.2.cloned.1.call-done = f32[128,1024]{1,0:T(8,128)} async-done(((f32[1024,1024]{1,0:T(8,128)}), f32[128,1024]{1,0:T(8,128)}) %reduce-scatter.2.cloned.1.call-update) | async-done | bytes 524304 | tf_op jit(solution)/shard_map/reduce_scatter | solution.py:41
  86.0 1.0 fusion.16
  86.9 0.0 copy-start.3
  86.9 1.3 fusion.19
  88.3 0.0 copy-done.5
  88.3 1.3 convolution_bitcast_fusion.1
  89.6 0.0 copy-start.6
  89.6 0.0 all-reduce.8.cloned.1.call-update
  89.6 0.0 copy-start.7
  89.6 0.0 all-reduce.10.cloned.1.call-start
  89.6 63.8 %all-reduce.8.cloned.1.call-done = (f32[512,512]{0,1:T(8,128)}, f32[512,512]{1,0:T(8,128)}) async-done(((f32[512,512]{0,1:T(8,128)}, f32[512,512]{1,0:T(8,128)}), (f32[512,512]{0,1:T(8,128)}, f32[512,512]{1,0:T(8,128)})) %all-reduce.8.cloned.1.call-update) | async-done | bytes 2097168 | tf_op jit(solution)/shard_map/psum | solution.py:10
  153.5 0.0 copy-start.8
  153.5 0.0 all-reduce.10.cloned.1.call-update
  153.5 0.0 all-reduce.6.cloned.1.call-start
  153.5 0.0 copy-done.6
  153.5 0.2 copy.14
  153.8 0.0 copy-done.7
  153.8 0.2 copy.15
  154.0 0.0 copy-done.3
  154.0 0.0 copy-done
  154.0 0.5 copy-done.8
  154.5 0.2 fusion.7
  154.7 0.0 copy-start.9
  154.7 1.3 fusion.20
  156.1 0.0 all-reduce.6.cloned.1.call-update
  156.1 69.6 %all-reduce.10.cloned.1.call-done = (f32[512,512]{0,1:T(8,128)}, f32[512,512]{1,0:T(8,128)}) async-done(((f32[512,512]{0,1:T(8,128)}, f32[512,512]{1,0:T(8,128)}), (f32[512,512]{0,1:T(8,128)}, f32[512,512]{1,0:T(8,128)})) %all-reduce.10.cloned.1.call-update) | async-done | bytes 2097168 | tf_op jit(solution)/shard_map/psum | solution.py:11
  225.7 0.0 copy-start.1
  225.7 0.0 copy-start.4
  225.7 1.5 fusion.14
  227.3 0.0 copy-done.9
  227.3 0.0 copy-done.1
  227.3 0.3 copy-done.4
  227.6 1.0 fusion.3
  228.6 0.0 copy-start.2
  228.6 132.8 %all-reduce.6.cloned.1.call-done = f32[512,512]{0,1:T(8,128)} async-done(((f32[512,512]{0,1:T(8,128)}), f32[512,512]{0,1:T(8,128)}) %all-reduce.6.cloned.1.call-update) | async-done | bytes 1048592 | tf_op jit(solution)/shard_map/psum | solution.py:55
  361.4 1.7 fusion.4
  363.1 1.0 copy.18
  364.1 0.0 copy-done.2
  364.1 1.0 copy.17
Async XLA Ops:
  7.2 146.8 %copy-start = (bf16[512,512]{1,0:T(8,128)(2,1)S(1)}, bf16[512,512]{1,0:T(8,128)(2,1)}, u32[]{:S(2)}) copy-start(bf16[512,512]{1,0:T(8,128)(2,1)} %param.12) | copy-start | bytes 1572868
  7.2 25.2 %copy-start.10 = (bf16[1024,4,1,128]{3,1,2,0:T(4,128)(2,1)S(1)}, bf16[1024,4,1,128]{3,1,2,0:T(4,128)(2,1)}, u32[]{:S(2)}) copy-start(bf16[1024,4,1,128]{3,1,2,0:T(4,128)(2,1)} %param.8) | copy-start | bytes 3145732
  7.2 78.8 %reduce-scatter.2.cloned.1.call-start = ((), (), s32[]{:S(2)}) async-start(), calls=%async_computation.1 | async-start | bytes 4718592 | tf_op jit(solution)/shard_map/reduce_scatter | solution.py:41
  35.6 52.7 %copy-start.5 = (bf16[128,512]{1,0:T(8,128)(2,1)S(1)}, bf16[128,512]{1,0:T(8,128)(2,1)}, u32[]{:S(2)}) copy-start(bf16[128,512]{1,0:T(8,128)(2,1)} %param.10) | copy-start | bytes 393220
  35.6 117.8 %all-reduce.8.cloned.1.call-start = ((), (), s32[]{:S(2)}) async-start(), calls=%async_computation.3 | async-start | bytes 4194304 | tf_op jit(solution)/shard_map/psum | solution.py:10
  86.9 67.1 %copy-start.3 = (bf16[128,512]{1,0:T(8,128)(2,1)}, bf16[128,512]{1,0:T(8,128)(2,1)S(1)}, u32[]{:S(2)}) copy-start(bf16[128,512]{1,0:T(8,128)(2,1)S(1)} %fusion.16) | copy-start | bytes 393220
  89.6 64.0 %copy-start.6 = (bf16[512,512]{1,0:T(8,128)(2,1)S(1)}, bf16[512,512]{1,0:T(8,128)(2,1)}, u32[]{:S(2)}) copy-start(bf16[512,512]{1,0:T(8,128)(2,1)} %param.14) | copy-start | bytes 1572868
  89.6 64.2 %copy-start.7 = (bf16[512,512]{1,0:T(8,128)(2,1)S(1)}, bf16[512,512]{1,0:T(8,128)(2,1)}, u32[]{:S(2)}) copy-start(bf16[512,512]{1,0:T(8,128)(2,1)} %param.15) | copy-start | bytes 1572868
  89.6 136.1 %all-reduce.10.cloned.1.call-start = ((), (), s32[]{:S(2)}) async-start(), calls=%async_computation.4 | async-start | bytes 4194304 | tf_op jit(solution)/shard_map/psum | solution.py:11
  153.5 1.0 copy-start.8
  153.5 207.9 %all-reduce.6.cloned.1.call-start = ((), (), s32[]{:S(2)}) async-start(), calls=%async_computation.2 | async-start | bytes 2097152 | tf_op jit(solution)/shard_map/psum | solution.py:55
  154.7 72.5 %copy-start.9 = (bf16[128,512]{1,0:T(8,128)(2,1)}, bf16[128,512]{1,0:T(8,128)(2,1)S(1)}, u32[]{:S(2)}) copy-start(bf16[128,512]{1,0:T(8,128)(2,1)S(1)} %fusion.7) | copy-start | bytes 393220
  225.7 1.6 copy-start.1
  225.7 1.9 copy-start.4
  228.6 135.5 %copy-start.2 = (bf16[512,512]{1,0:T(8,128)(2,1)}, bf16[512,512]{1,0:T(8,128)(2,1)S(1)}, u32[]{:S(2)}) copy-start(bf16[512,512]{1,0:T(8,128)(2,1)S(1)} %fusion.3) | copy-start | bytes 1572868
Sparse Core Ops, SparseCore 0:
  35.7 50.1 reduce-scatter.1
  89.7 63.7 all-reduce.7
  156.5 69.1 all-reduce.9
  230.8 130.6 all-reduce.5
